TPU v7x, 128 devices: a whole 4x4x4 slice. The times are simulated.
128 devices in a mesh: sensor: 32 (over z, y, core), rows: 4 (over x).
Axes of the slice: x: 4, y: 4, z: 4, core: 2. Of those that a mesh axis runs over, the one named last changes fastest.
Arguments:
- photon_charge: bfloat16 [128, 128, 3, 32], P(('sensor', 'rows')), may hold values from 20 to 400
- photon_pixel: int32 [128, 128, 32], P(('sensor', 'rows')), may hold values from 0 to 524287
- photon_count: int32 [128, 128], P(('sensor', 'rows')), may hold values from 0 to 32, as said below
- diffusion_kernel: bfloat16 [3, 21, 21], replicated, may hold values from 0.00045204163 to 0.009033203
- fatter_kernel: bfloat16 [21, 21], replicated, may hold values from 4.529953e-05 to 0.00090408325
- crosstalk: bfloat16 [32, 16, 16], replicated, may hold values from -0.125 to 1.1875
Outputs:
- amplifier_images: float32 [32, 16, 4, 64, 512], P(None, None, 'rows', 'sensor')
Inputs may be any that keep to these rules, and one draw needn't show every extreme that they name: Slots 0 to photon_count[i, d] - 1 of block (i, d) are live, the others are ignored. At most 2048 live slots in all reach one owner device.
All inputs are finite; a program needn't handle non-finite values.
Results may differ from a plain program's by a relative error of at most 0.0085.
Values may be sent and summed in bfloat16 or wider, within the bound.
A program may use at most 64 MiB of HBM per device.

v0:
```python
import jax
import jax.numpy as jnp
from jax import lax
from jax.sharding import PartitionSpec as P

COLS = 4096
KSIZE = 21
READ_ROWS = 64


def extended_2(block, sides, width):
    for axis, dim in sides:
        count = lax.axis_size(axis)
        forward = [(i, i + 1) for i in range(count - 1)]
        backward = [(target, source) for source, target in forward]
        low = lax.ppermute(
            lax.slice_in_dim(block, block.shape[dim] - width, None, axis=dim), axis, forward
        )
        high = lax.ppermute(lax.slice_in_dim(block, 0, width, axis=dim), axis, backward)
        block = jnp.concatenate([low, block, high], axis=dim)
    return block


def seam_fill(extended, interior, rim_width, band_last):
    inner = interior.shape[2]
    mirror = jnp.flip(interior[:, ::-1, inner - rim_width :, :], axis=2)
    lower = jnp.where(band_last, mirror, extended[:, :, inner + rim_width :, :])
    return jnp.concatenate([extended[:, :, : inner + rim_width, :], lower], axis=2)


def convolve(extended, kernel, out_rows):
    size_k = kernel.shape[-1]
    half_k = size_k // 2
    tile_width = 128
    channels = extended.shape[0]
    rows_in = extended.shape[2]
    columns = extended.shape[3]
    tile_count = columns // tile_width
    window_span = tile_width + size_k - 1
    padded = jnp.pad(extended, ((0, 0), (0, 0), (0, 0), (half_k, tile_width - half_k)))
    head_part = padded[..., :columns].reshape(channels, 2, rows_in, tile_count, tile_width)
    tail_part = padded[..., tile_width : tile_width + columns].reshape(
        channels, 2, rows_in, tile_count, tile_width
    )[..., : size_k - 1]
    windows = jnp.concatenate([head_part, tail_part], axis=-1)
    offsets = (
        jnp.arange(window_span, dtype=jnp.int32)[:, None]
        - jnp.arange(tile_width, dtype=jnp.int32)[None, :]
    )
    selector = (offsets[None] == jnp.arange(size_k, dtype=jnp.int32)[:, None, None]).astype(
        jnp.float32
    )
    toeplitz = jnp.einsum("hcab,bwo->ahcwo", kernel.astype(jnp.float32), selector).astype(
        jnp.bfloat16
    )

    def add_row(offset_row, summed):
        row_slab = lax.dynamic_slice_in_dim(windows, offset_row, out_rows, 2)
        matrix = lax.dynamic_index_in_dim(toeplitz, offset_row, 0, keepdims=False)
        return summed + jnp.einsum(
            "chrnw,hcwo->hrno", row_slab, matrix, preferred_element_type=jnp.float32
        )

    summed = lax.fori_loop(
        0, size_k, add_row, jnp.zeros((2, out_rows, tile_count, tile_width), jnp.float32)
    )
    return summed.reshape(2, out_rows, columns)


def bin_photons(photons, spot_index, row_map, row_total, columns):
    depths = photons.shape[0]
    photon_total = photons.shape[1]
    step_size = min(photon_total, 1024)
    step_count = photon_total // step_size

    def bin_block(block_index, summed):
        charge_part = lax.dynamic_slice_in_dim(photons, block_index * step_size, step_size, 1)
        located = lax.dynamic_slice_in_dim(spot_index, block_index * step_size, step_size, 0)
        target_row = row_map(located // columns)
        column = located % columns
        row_hot = (target_row[None, :] == jnp.arange(row_total, dtype=jnp.int32)[:, None]).astype(
            jnp.bfloat16
        )
        weighted = (charge_part[:, None, :] * row_hot[None]).reshape(depths * row_total, step_size)
        col_hot = (column[:, None] == jnp.arange(columns, dtype=jnp.int32)[None, :]).astype(
            jnp.bfloat16
        )
        return summed + jnp.dot(weighted, col_hot, preferred_element_type=jnp.float32)

    return lax.fori_loop(
        0, step_count, bin_block, jnp.zeros((depths * row_total, columns), jnp.float32)
    )


def shards(photon_charge, photon_pixel, photon_count, diffusion_kernel, fatter_kernel, crosstalk):
    sensor_count = lax.axis_size("sensor")
    band_count = lax.axis_size("rows")
    device_count = sensor_count * band_count
    slot_count = photon_charge.shape[3]
    depths = photon_charge.shape[2]
    charge = photon_charge[0]
    pixels = photon_pixel[0]
    counts = photon_count[0]
    live_slot = jnp.arange(slot_count, dtype=jnp.int32)[None, :] < counts[:, None]
    charge = jnp.where(live_slot[:, None, :], charge, jnp.zeros((), jnp.bfloat16))
    count_column = counts.reshape(device_count, 1)
    got_charge, got_pixel, got_count = (
        lax.all_to_all(charge, ("sensor", "rows"), split_axis=0, concat_axis=0, tiled=True),
        lax.all_to_all(pixels, ("sensor", "rows"), split_axis=0, concat_axis=0, tiled=True),
        lax.all_to_all(count_column, ("sensor", "rows"), split_axis=0, concat_axis=0, tiled=True),
    )
    slot_total = device_count * slot_count
    flat_charge = jnp.transpose(got_charge, (1, 0, 2)).reshape(depths, slot_total)
    flat_pixel = got_pixel.reshape(slot_total)
    read_rows = READ_ROWS
    columns = COLS

    def same_row(pixel_row):
        return pixel_row

    binned = bin_photons(flat_charge, flat_pixel, same_row, 2 * read_rows, columns)
    binned = binned.reshape(depths, 2, read_rows, columns).astype(jnp.bfloat16)
    diffusion_pair = jnp.stack([diffusion_kernel, jnp.flip(diffusion_kernel, axis=1)])
    fatter_pair = jnp.stack([fatter_kernel, jnp.flip(fatter_kernel, axis=0)])[:, None]
    half_width = KSIZE // 2
    band_index = lax.axis_index("rows")
    band_last = band_index == band_count - 1
    extended = extended_2(binned, (("rows", 2),), half_width)
    extended = seam_fill(extended, binned, half_width, band_last)
    diffused = convolve(extended, diffusion_pair, read_rows).astype(jnp.bfloat16)
    diffused_rim = extended_2(diffused[None], (("rows", 2),), half_width)
    diffused_ext = seam_fill(diffused_rim, diffused[None], half_width, band_last)[0]
    potential = convolve(diffused_ext[None], fatter_pair, read_rows)
    final = diffused.astype(jnp.float32) * (1.0 - potential)
    seg_width = columns // 8
    segments = final.reshape(2, read_rows, 8, seg_width)
    odd_segment = (jnp.arange(8, dtype=jnp.int32) % 2 == 1)[None, None, :, None]
    segments = jnp.where(odd_segment, jnp.flip(segments, axis=3), segments)
    amplifiers = (
        jnp.transpose(segments, (0, 2, 1, 3)).reshape(16, read_rows, seg_width).astype(jnp.bfloat16)
    )
    mixed = jnp.einsum(
        "sij,sjrc->sirc",
        crosstalk,
        lax.all_to_all(amplifiers[None], "sensor", split_axis=2, concat_axis=0, tiled=True),
        preferred_element_type=jnp.float32,
    )
    return mixed.reshape(sensor_count, 16, 1, read_rows // sensor_count, seg_width)


def solution(mesh):
    placed = (
        P(("sensor", "rows"), None, None, None),
        P(("sensor", "rows"), None, None),
        P(("sensor", "rows"), None),
        P(),
        P(),
        P(),
    )
    return jax.shard_map(
        shards,
        mesh=mesh,
        in_specs=placed,
        out_specs=P(None, None, "rows", "sensor", None),
        check_vma=False,
    )
```

profile of v0, /device:TPU:7, one launch (start us, length us, event | category | flops | bytes accessed | tf_op | source)
XLA Modules:
  0.0 361.5 jit_solution(13160880546895546684)
XLA Ops:
  1.4 10.8 %all-to-all-start.1 = ((s32[128,1,32]{2,1,0:T(1,128)}), s32[128,1,32]{2,1,0:T(1,128)S(1)}, u32[]{:S(2)}, u32[]{:S(2)}) async-start(s32[128,1,32]{2,1,0:T(1,128)} %bitcast.3), calls=%async_computation.1 | async-start | bytes 131072 | tf_op jit(solution)/shard_map/all_to_all | solution.py:109
  14.6 5.8 %all-to-all-done.1 = s32[128,1,32]{2,1,0:T(1,128)S(1)} async-done(((s32[128,1,32]{2,1,0:T(1,128)}), s32[128,1,32]{2,1,0:T(1,128)S(1)}, u32[]{:S(2)}, u32[]{:S(2)}) %all-to-all-start.1) | async-done | bytes 16416 | tf_op jit(solution)/shard_map/all_to_all | solution.py:109
  20.3 5.8 %all-to-all-start = ((bf16[128,3,32]{2,1,0:T(4,128)(2,1)}), bf16[128,3,32]{2,1,0:T(4,128)(2,1)S(1)}, u32[]{:S(2)}, u32[]{:S(2)}) async-start(bf16[128,3,32]{2,1,0:T(4,128)(2,1)} %bitcast_select_fusion), calls=%async_computation | async-start | bytes 262144 | tf_op jit(solution)/shard_map/all_to_all | solution.py:108
  27.7 6.8 %all-to-all-done = bf16[128,3,32]{2,1,0:T(4,128)(2,1)S(1)} async-done(((bf16[128,3,32]{2,1,0:T(4,128)(2,1)}), bf16[128,3,32]{2,1,0:T(4,128)(2,1)S(1)}, u32[]{:S(2)}, u32[]{:S(2)}) %all-to-all-start) | async-done | bytes 24608 | tf_op jit(solution)/shard_map/all_to_all | solution.py:108
  34.7 30.9 %while.44 = (s32[]{:T(128)}, f32[384,4096]{1,0:T(8,128)}, bf16[3,4096]{1,0:T(4,128)(2,1)S(1)}, s32[4096]{0:T(1024)S(1)}, s32[]{:T(128)}, /*index=5*/s32[]{:T(128)}, s32[]{:T(128)}, s32[]{:T(128)}) while((s32[]{:T(128)}, f32[384,4096]{1,0:T(8,128)}, bf16[3,4096]{1,0:T(4,128)(2,1)S(1)}, s32[4096]{0:T(1024)S(1)}, s32[]{:T(128)}, ...), condition=%wide.region_1.2_spmd.clone, body=%wide.region_0.1_spmd.clone.sunk | while | flops 3229243392 | bytes 14725273 | solution.py:90
  34.9 6.1 %select_add_fusion.4 = f32[384,4096]{1,0:T(8,128)} fusion(f32[384,4096]{1,0:T(8,128)} %get-tuple-element.478, bf16[384,1024]{1,0:T(8,128)(2,1)S(1)} %bitcast.93, s32[1024]{0:T(1024)S(1)} %get-tuple-element.460, pred[]{:T(512)S(6)} %compare.103), kind=kOutput, calls=%fused_computation.3.clone.1 | convolution fusion | flops 3228565504 | bytes 13373441 | tf_op jit(solution)/shard_map/while/body/eval_jaxpr/dot_general | solution.py:88
  41.2 8.0 %select_add_fusion.4 = f32[384,4096]{1,0:T(8,128)} fusion(f32[384,4096]{1,0:T(8,128)} %get-tuple-element.478, bf16[384,1024]{1,0:T(8,128)(2,1)S(1)} %bitcast.93, s32[1024]{0:T(1024)S(1)} %get-tuple-element.460, pred[]{:T(512)S(6)} %compare.103), kind=kOutput, calls=%fused_computation.3.clone.1 | convolution fusion | flops 3228565504 | bytes 13373441 | tf_op jit(solution)/shard_map/while/body/eval_jaxpr/dot_general | solution.py:88
  49.4 8.0 %select_add_fusion.4 = f32[384,4096]{1,0:T(8,128)} fusion(f32[384,4096]{1,0:T(8,128)} %get-tuple-element.478, bf16[384,1024]{1,0:T(8,128)(2,1)S(1)} %bitcast.93, s32[1024]{0:T(1024)S(1)} %get-tuple-element.460, pred[]{:T(512)S(6)} %compare.103), kind=kOutput, calls=%fused_computation.3.clone.1 | convolution fusion | flops 3228565504 | bytes 13373441 | tf_op jit(solution)/shard_map/while/body/eval_jaxpr/dot_general | solution.py:88
  57.6 8.0 %select_add_fusion.4 = f32[384,4096]{1,0:T(8,128)} fusion(f32[384,4096]{1,0:T(8,128)} %get-tuple-element.478, bf16[384,1024]{1,0:T(8,128)(2,1)S(1)} %bitcast.93, s32[1024]{0:T(1024)S(1)} %get-tuple-element.460, pred[]{:T(512)S(6)} %compare.103), kind=kOutput, calls=%fused_computation.3.clone.1 | convolution fusion | flops 3228565504 | bytes 13373441 | tf_op jit(solution)/shard_map/while/body/eval_jaxpr/dot_general | solution.py:88
  73.8 4.8 %collective-permute-start.1 = (bf16[3,2,10,4096]{3,1,2,0:T(2,128)(2,1)}, bf16[3,2,10,4096]{3,1,2,0:T(2,128)(2,1)}, u32[]{:S(2)}, u32[]{:S(2)}) collective-permute-start(bf16[3,2,10,4096]{3,1,2,0:T(2,128)(2,1)} %copy.40), channel_id=1, source_target_pairs={{1,0},{2,1},{3,2},{5,4},{6,5},{7,6},{9,8},{10,9},{11,10},{13,12},{... | collective-permute-start | bytes 1474568 | tf_op jit(solution)/shard_map/ppermute | solution.py:19
  83.8 15.4 %rev.22 = bf16[3,2,10,4096]{3,2,1,0:T(8,128)(2,1)} reverse(bf16[3,2,10,4096]{3,2,1,0:T(8,128)(2,1)} %copy-done.2), dimensions={1,2} | reverse | bytes 983040 | tf_op jit(solution)/shard_map/jit(_flip)/rev | solution.py:26
  110.0 6.7 %reshape.160 = bf16[3,2,84,32,128]{4,3,2,1,0:T(8,128)(2,1)} reshape(bf16[3,2,84,4096]{3,2,1,0:T(8,128)(2,1)} %get-tuple-element.383) | data formatting | bytes 8257536 | tf_op jit(solution)/shard_map/reshape | solution.py:42
  116.6 6.6 %reshape.159 = bf16[3,2,84,32,128]{4,3,2,1,0:T(8,128)(2,1)} reshape(bf16[3,2,84,4096]{3,2,1,0:T(8,128)(2,1)} %get-tuple-element.382) | data formatting | bytes 8257536 | tf_op jit(solution)/shard_map/reshape | solution.py:41
  123.3 9.1 %pad_maximum_fusion = bf16[3,2,84,32,148]{4,3,2,1,0:T(8,128)(2,1)} fusion(bf16[3,2,84,32,20]{4,3,2,1,0:T(8,128)(2,1)} %bitcast.94, bf16[3,2,84,32,128]{4,3,2,1,0:T(8,128)(2,1)} %reshape.159), kind=kLoop, calls=%fused_computation.33 | loop fusion | flops 9547776 | bytes 9547776 | tf_op jit(solution)/shard_map/concatenate | solution.py:45
  132.4 100.6 %while.45 = (s32[]{:T(128)}, f32[2,64,32,128]{3,2,1,0:T(8,128)S(1)}, bf16[3,2,84,32,148]{4,3,2,1,0:T(8,128)(2,1)}, bf16[21,2,3,148,128]{4,3,2,1,0:T(8,128)(2,1)}, s32[]{:T(128)}, /*index=5*/s32[]{:T(128)}) while((s32[]{:T(128)}, f32[2,64,32,128]{3,2,1,0:T(8,128)S(1)}, bf16[3,2,84,32,148]{4,3,2,1,0:T(8,128)(2,1)}, ...), condition=%wide.region_3.4_spmd.clone, body=%wide.region_2.3_spmd.clone.sunk | while | flops 466616320 | bytes 10720335 | solution.py:64
  151.6 4.8 %bitcast_add_fusion.2 = f32[2,64,32,128]{3,2,1,0:T(8,128)S(1)} fusion(f32[2,64,32,128]{3,2,1,0:T(8,128)S(1)} %get-tuple-element.500, pred[]{:T(512)S(6)} %compare.104, bf16[21,2,3,148,128]{4,3,2,1,0:T(8,128)(2,1)} %get-tuple-element.508, s32[]{:T(128)} %get-tuple-element.499, bf16[3,2,84,32,148]{4,3,2,1,0:T(8,128)(2,1)} %get-tuple-element.507), kind=kOutput, calls=%fused_computation.18.clone.1 | convolution fusion | flops 466616320 | bytes 10720257 | tf_op jit(solution)/shard_map/while/body/eval_jaxpr/chrnw,hcwo->hrno/dot_general | solution.py:60
  156.4 4.8 %bitcast_add_fusion.2 = f32[2,64,32,128]{3,2,1,0:T(8,128)S(1)} fusion(f32[2,64,32,128]{3,2,1,0:T(8,128)S(1)} %get-tuple-element.500, pred[]{:T(512)S(6)} %compare.104, bf16[21,2,3,148,128]{4,3,2,1,0:T(8,128)(2,1)} %get-tuple-element.508, s32[]{:T(128)} %get-tuple-element.499, bf16[3,2,84,32,148]{4,3,2,1,0:T(8,128)(2,1)} %get-tuple-element.507), kind=kOutput, calls=%fused_computation.18.clone.1 | convolution fusion | flops 466616320 | bytes 10720257 | tf_op jit(solution)/shard_map/while/body/eval_jaxpr/chrnw,hcwo->hrno/dot_general | solution.py:60
  161.2 4.8 %bitcast_add_fusion.2 = f32[2,64,32,128]{3,2,1,0:T(8,128)S(1)} fusion(f32[2,64,32,128]{3,2,1,0:T(8,128)S(1)} %get-tuple-element.500, pred[]{:T(512)S(6)} %compare.104, bf16[21,2,3,148,128]{4,3,2,1,0:T(8,128)(2,1)} %get-tuple-element.508, s32[]{:T(128)} %get-tuple-element.499, bf16[3,2,84,32,148]{4,3,2,1,0:T(8,128)(2,1)} %get-tuple-element.507), kind=kOutput, calls=%fused_computation.18.clone.1 | convolution fusion | flops 466616320 | bytes 10720257 | tf_op jit(solution)/shard_map/while/body/eval_jaxpr/chrnw,hcwo->hrno/dot_general | solution.py:60
  166.0 4.8 %bitcast_add_fusion.2 = f32[2,64,32,128]{3,2,1,0:T(8,128)S(1)} fusion(f32[2,64,32,128]{3,2,1,0:T(8,128)S(1)} %get-tuple-element.500, pred[]{:T(512)S(6)} %compare.104, bf16[21,2,3,148,128]{4,3,2,1,0:T(8,128)(2,1)} %get-tuple-element.508, s32[]{:T(128)} %get-tuple-element.499, bf16[3,2,84,32,148]{4,3,2,1,0:T(8,128)(2,1)} %get-tuple-element.507), kind=kOutput, calls=%fused_computation.18.clone.1 | convolution fusion | flops 466616320 | bytes 10720257 | tf_op jit(solution)/shard_map/while/body/eval_jaxpr/chrnw,hcwo->hrno/dot_general | solution.py:60
  170.7 4.8 %bitcast_add_fusion.2 = f32[2,64,32,128]{3,2,1,0:T(8,128)S(1)} fusion(f32[2,64,32,128]{3,2,1,0:T(8,128)S(1)} %get-tuple-element.500, pred[]{:T(512)S(6)} %compare.104, bf16[21,2,3,148,128]{4,3,2,1,0:T(8,128)(2,1)} %get-tuple-element.508, s32[]{:T(128)} %get-tuple-element.499, bf16[3,2,84,32,148]{4,3,2,1,0:T(8,128)(2,1)} %get-tuple-element.507), kind=kOutput, calls=%fused_computation.18.clone.1 | convolution fusion | flops 466616320 | bytes 10720257 | tf_op jit(solution)/shard_map/while/body/eval_jaxpr/chrnw,hcwo->hrno/dot_general | solution.py:60
  175.5 4.8 %bitcast_add_fusion.2 = f32[2,64,32,128]{3,2,1,0:T(8,128)S(1)} fusion(f32[2,64,32,128]{3,2,1,0:T(8,128)S(1)} %get-tuple-element.500, pred[]{:T(512)S(6)} %compare.104, bf16[21,2,3,148,128]{4,3,2,1,0:T(8,128)(2,1)} %get-tuple-element.508, s32[]{:T(128)} %get-tuple-element.499, bf16[3,2,84,32,148]{4,3,2,1,0:T(8,128)(2,1)} %get-tuple-element.507), kind=kOutput, calls=%fused_computation.18.clone.1 | convolution fusion | flops 466616320 | bytes 10720257 | tf_op jit(solution)/shard_map/while/body/eval_jaxpr/chrnw,hcwo->hrno/dot_general | solution.py:60
  180.3 4.8 %bitcast_add_fusion.2 = f32[2,64,32,128]{3,2,1,0:T(8,128)S(1)} fusion(f32[2,64,32,128]{3,2,1,0:T(8,128)S(1)} %get-tuple-element.500, pred[]{:T(512)S(6)} %compare.104, bf16[21,2,3,148,128]{4,3,2,1,0:T(8,128)(2,1)} %get-tuple-element.508, s32[]{:T(128)} %get-tuple-element.499, bf16[3,2,84,32,148]{4,3,2,1,0:T(8,128)(2,1)} %get-tuple-element.507), kind=kOutput, calls=%fused_computation.18.clone.1 | convolution fusion | flops 466616320 | bytes 10720257 | tf_op jit(solution)/shard_map/while/body/eval_jaxpr/chrnw,hcwo->hrno/dot_general | solution.py:60
  185.1 4.8 %bitcast_add_fusion.2 = f32[2,64,32,128]{3,2,1,0:T(8,128)S(1)} fusion(f32[2,64,32,128]{3,2,1,0:T(8,128)S(1)} %get-tuple-element.500, pred[]{:T(512)S(6)} %compare.104, bf16[21,2,3,148,128]{4,3,2,1,0:T(8,128)(2,1)} %get-tuple-element.508, s32[]{:T(128)} %get-tuple-element.499, bf16[3,2,84,32,148]{4,3,2,1,0:T(8,128)(2,1)} %get-tuple-element.507), kind=kOutput, calls=%fused_computation.18.clone.1 | convolution fusion | flops 466616320 | bytes 10720257 | tf_op jit(solution)/shard_map/while/body/eval_jaxpr/chrnw,hcwo->hrno/dot_general | solution.py:60
  189.9 4.8 %bitcast_add_fusion.2 = f32[2,64,32,128]{3,2,1,0:T(8,128)S(1)} fusion(f32[2,64,32,128]{3,2,1,0:T(8,128)S(1)} %get-tuple-element.500, pred[]{:T(512)S(6)} %compare.104, bf16[21,2,3,148,128]{4,3,2,1,0:T(8,128)(2,1)} %get-tuple-element.508, s32[]{:T(128)} %get-tuple-element.499, bf16[3,2,84,32,148]{4,3,2,1,0:T(8,128)(2,1)} %get-tuple-element.507), kind=kOutput, calls=%fused_computation.18.clone.1 | convolution fusion | flops 466616320 | bytes 10720257 | tf_op jit(solution)/shard_map/while/body/eval_jaxpr/chrnw,hcwo->hrno/dot_general | solution.py:60
  194.7 4.8 %bitcast_add_fusion.2 = f32[2,64,32,128]{3,2,1,0:T(8,128)S(1)} fusion(f32[2,64,32,128]{3,2,1,0:T(8,128)S(1)} %get-tuple-element.500, pred[]{:T(512)S(6)} %compare.104, bf16[21,2,3,148,128]{4,3,2,1,0:T(8,128)(2,1)} %get-tuple-element.508, s32[]{:T(128)} %get-tuple-element.499, bf16[3,2,84,32,148]{4,3,2,1,0:T(8,128)(2,1)} %get-tuple-element.507), kind=kOutput, calls=%fused_computation.18.clone.1 | convolution fusion | flops 466616320 | bytes 10720257 | tf_op jit(solution)/shard_map/while/body/eval_jaxpr/chrnw,hcwo->hrno/dot_general | solution.py:60
  199.5 4.8 %bitcast_add_fusion.2 = f32[2,64,32,128]{3,2,1,0:T(8,128)S(1)} fusion(f32[2,64,32,128]{3,2,1,0:T(8,128)S(1)} %get-tuple-element.500, pred[]{:T(512)S(6)} %compare.104, bf16[21,2,3,148,128]{4,3,2,1,0:T(8,128)(2,1)} %get-tuple-element.508, s32[]{:T(128)} %get-tuple-element.499, bf16[3,2,84,32,148]{4,3,2,1,0:T(8,128)(2,1)} %get-tuple-element.507), kind=kOutput, calls=%fused_computation.18.clone.1 | convolution fusion | flops 466616320 | bytes 10720257 | tf_op jit(solution)/shard_map/while/body/eval_jaxpr/chrnw,hcwo->hrno/dot_general | solution.py:60
  204.3 4.8 %bitcast_add_fusion.2 = f32[2,64,32,128]{3,2,1,0:T(8,128)S(1)} fusion(f32[2,64,32,128]{3,2,1,0:T(8,128)S(1)} %get-tuple-element.500, pred[]{:T(512)S(6)} %compare.104, bf16[21,2,3,148,128]{4,3,2,1,0:T(8,128)(2,1)} %get-tuple-element.508, s32[]{:T(128)} %get-tuple-element.499, bf16[3,2,84,32,148]{4,3,2,1,0:T(8,128)(2,1)} %get-tuple-element.507), kind=kOutput, calls=%fused_computation.18.clone.1 | convolution fusion | flops 466616320 | bytes 10720257 | tf_op jit(solution)/shard_map/while/body/eval_jaxpr/chrnw,hcwo->hrno/dot_general | solution.py:60
  243.7 10.0 %rev.24 = bf16[1,2,10,4096]{3,2,1,0:T(8,128)(2,1)} reverse(bf16[1,2,10,4096]{3,2,1,0:T(8,128)(2,1)S(1)} %get-tuple-element.389), dimensions={1,2} | reverse | bytes 327680 | tf_op jit(solution)/shard_map/jit(_flip)/rev | solution.py:26
  255.9 6.0 %collective-permute-done.2 = bf16[1,2,10,4096]{3,2,1,0:T(8,128)(2,1)S(1)} collective-permute-done((bf16[1,2,10,4096]{3,2,1,0:T(8,128)(2,1)S(1)}, bf16[1,2,10,4096]{3,2,1,0:T(8,128)(2,1)S(1)}, u32[]{:S(2)}, u32[]{:S(2)}) %collective-permute-start.2) | collective-permute-done | bytes 163872 | tf_op jit(solution)/shard_map/ppermute | solution.py:16
  272.7 57.3 %while.46 = (s32[]{:T(128)}, f32[2,64,32,128]{3,2,1,0:T(8,128)S(1)}, bf16[1,2,84,32,148]{4,3,2,1,0:T(8,128)(2,1)}, bf16[21,2,1,148,128]{4,3,1,2,0:T(8,128)(2,1)}, s32[]{:T(128)}, /*index=5*/s32[]{:T(128)}) while((s32[]{:T(128)}, f32[2,64,32,128]{3,2,1,0:T(8,128)S(1)}, bf16[1,2,84,32,148]{4,3,2,1,0:T(8,128)(2,1)}, ...), condition=%wide.region_5.6_spmd.clone, body=%wide.region_4.5_spmd.clone.sunk | while | flops 156237824 | bytes 6370383 | solution.py:64
  335.0 6.0 %all-to-all-start.2 = ((bf16[1,16,64,512]{3,1,0,2:T(8,128)(2,1)}), bf16[1,16,64,512]{3,1,0,2:T(8,128)(2,1)S(1)}, u32[]{:S(2)}, u32[]{:S(2)}) async-start(bf16[1,16,64,512]{3,1,0,2:T(8,128)(2,1)} %fusion.39), calls=%async_computation.2 | async-start | bytes 2097152 | tf_op jit(solution)/shard_map/all_to_all | solution.py:145
  341.1 17.0 %all-to-all-done.2 = bf16[1,16,64,512]{3,1,0,2:T(8,128)(2,1)S(1)} async-done(((bf16[1,16,64,512]{3,1,0,2:T(8,128)(2,1)}), bf16[1,16,64,512]{3,1,0,2:T(8,128)(2,1)S(1)}, u32[]{:S(2)}, u32[]{:S(2)}) %all-to-all-start.2) | async-done | bytes 1048608 | tf_op jit(solution)/shard_map/all_to_all | solution.py:145
  (113 shorter events, 162.1 us)
Async XLA Ops:
  1.4 18.9 %all-to-all-start.1 = ((s32[128,1,32]{2,1,0:T(1,128)}), s32[128,1,32]{2,1,0:T(1,128)S(1)}, u32[]{:S(2)}, u32[]{:S(2)}) async-start(s32[128,1,32]{2,1,0:T(1,128)} %bitcast.3), calls=%async_computation.1 | async-start | bytes 131072 | tf_op jit(solution)/shard_map/all_to_all | solution.py:109
  20.3 14.2 %all-to-all-start = ((bf16[128,3,32]{2,1,0:T(4,128)(2,1)}), bf16[128,3,32]{2,1,0:T(4,128)(2,1)S(1)}, u32[]{:S(2)}, u32[]{:S(2)}) async-start(bf16[128,3,32]{2,1,0:T(4,128)(2,1)} %bitcast_select_fusion), calls=%async_computation | async-start | bytes 262144 | tf_op jit(solution)/shard_map/all_to_all | solution.py:108
  68.8 9.8 %copy-start.3 = (bf16[3,21,21]{2,1,0:T(8,128)(2,1)S(1)}, bf16[3,21,21]{2,1,0:T(8,128)(2,1)}, u32[]{:S(2)}) copy-start(bf16[3,21,21]{2,1,0:T(8,128)(2,1)} %param.15) | copy-start | bytes 7942
  69.0 0.9 copy-start.2
  71.2 28.0 %collective-permute-start = (bf16[3,2,10,4096]{3,1,2,0:T(2,128)(2,1)}, bf16[3,2,10,4096]{3,1,2,0:T(2,128)(2,1)}, u32[]{:S(2)}, u32[]{:S(2)}) collective-permute-start(bf16[3,2,10,4096]{3,1,2,0:T(2,128)(2,1)} %copy.39), channel_id=1, source_target_pairs={{0,1},{1,2},{2,3},{4,5},{5,6},{6,7},{8,9},{9,10},{10,11},{12,13},{... | collective-permute-start | bytes 1474568 | tf_op jit(solution)/shard_map/ppermute | solution.py:16
  73.8 26.7 %collective-permute-start.1 = (bf16[3,2,10,4096]{3,1,2,0:T(2,128)(2,1)}, bf16[3,2,10,4096]{3,1,2,0:T(2,128)(2,1)}, u32[]{:S(2)}, u32[]{:S(2)}) collective-permute-start(bf16[3,2,10,4096]{3,1,2,0:T(2,128)(2,1)} %copy.40), channel_id=1, source_target_pairs={{1,0},{2,1},{3,2},{5,4},{6,5},{7,6},{9,8},{10,9},{11,10},{13,12},{... | collective-permute-start | bytes 1474568 | tf_op jit(solution)/shard_map/ppermute | solution.py:19
  80.2 3.6 copy-start.5
  123.3 9.1 %copy-start = (f32[2,64,32,128]{3,2,1,0:T(8,128)S(1)}, f32[2,64,32,128]{3,2,1,0:T(8,128)}, u32[]{:S(2)}) copy-start(f32[2,64,32,128]{3,2,1,0:T(8,128)} %custom-call.1) | copy-start | bytes 6291460
  233.0 3.7 %copy-start.1 = (f32[2,64,32,128]{3,2,1,0:T(8,128)}, f32[2,64,32,128]{3,2,1,0:T(8,128)S(1)}, u32[]{:S(2)}) copy-start(f32[2,64,32,128]{3,2,1,0:T(8,128)S(1)} %get-tuple-element.277) | copy-start | bytes 6291460
  236.7 18.2 %collective-permute-start.3 = (bf16[1,2,10,4096]{3,2,1,0:T(8,128)(2,1)}, bf16[1,2,10,4096]{3,2,1,0:T(8,128)(2,1)}, u32[]{:S(2)}, u32[]{:S(2)}) collective-permute-start(bf16[1,2,10,4096]{3,2,1,0:T(8,128)(2,1)} %get-tuple-element.388), channel_id=1, source_target_pairs={{1,0},{2,1},{3,2},{5,4},{6,5},{7,6},{9,8},{10,9},{11,10},{13,12},{... | collective-permute-start | bytes 491528 | tf_op jit(solution)/shard_map/ppermute | solution.py:19
  253.7 8.2 %collective-permute-start.2 = (bf16[1,2,10,4096]{3,2,1,0:T(8,128)(2,1)S(1)}, bf16[1,2,10,4096]{3,2,1,0:T(8,128)(2,1)S(1)}, u32[]{:S(2)}, u32[]{:S(2)}) collective-permute-start(bf16[1,2,10,4096]{3,2,1,0:T(8,128)(2,1)S(1)} %get-tuple-element.389), channel_id=1, source_target_pairs={{0,1},{1,2},{2,3},{4,5},{5,6},{6,7},{8,9},{9,10},{10,11},{12,13},{... | collective-permute-start | bytes 491528 | tf_op jit(solution)/shard_map/ppermute | solution.py:16
  333.8 7.1 %copy-start.4 = (bf16[32,16,16]{0,2,1:T(8,128)(2,1)S(1)}, bf16[32,16,16]{0,2,1:T(8,128)(2,1)}, u32[]{:S(2)}) copy-start(bf16[32,16,16]{0,2,1:T(8,128)(2,1)} %param.17) | copy-start | bytes 49156
  335.0 23.1 %all-to-all-start.2 = ((bf16[1,16,64,512]{3,1,0,2:T(8,128)(2,1)}), bf16[1,16,64,512]{3,1,0,2:T(8,128)(2,1)S(1)}, u32[]{:S(2)}, u32[]{:S(2)}) async-start(bf16[1,16,64,512]{3,1,0,2:T(8,128)(2,1)} %fusion.39), calls=%async_computation.2 | async-start | bytes 2097152 | tf_op jit(solution)/shard_map/all_to_all | solution.py:145
where the time goes:
time: 365 us; the launch traced here: 361 us
  matrix products  191 us (52%)
  local copies, waits for them, and re-layouts  70.5 us (19%)
  waiting for transfers between devices  35.5 us (10%)
  starting transfers between devices  31.9 us (9%)
  other arithmetic  31.4 us (9%)
    dot_general x42, matrix products, add_row(): jnp.einsum('chrnw,hcwo->hrno', row_slab, matrix, preferred_element_type=j...  157 us
    dot_general x4, matrix products, bin_block(): jnp.dot(weighted, col_hot, preferred_element_type=jnp.float32)  30.1 us
    rev x2, local copies, waits for them, and re-layouts, seam_fill(): mirror = jnp.flip(interior[:, ::-1, inner - rim_width:, :], axis=2)  25.4 us
    all_to_all x1, waiting for transfers between devices, shards(): lax.all_to_all(amplifiers[None], 'sensor', split_axis=2, concat_axis=0, t...  17 us
    concatenate x2, other arithmetic, convolve(): windows = jnp.concatenate([head_part, tail_part], axis=-1)  13.2 us
    all_to_all x1, starting transfers between devices, shards(): lax.all_to_all(pixels, ('sensor', 'rows'), split_axis=0, concat_axis=0, t...  10.8 us
    unnamed x17, local copies, waits for them, and re-layouts  10 us
    reshape x2, local copies, waits for them, and re-layouts, convolve(): padded[..., tile_width:tile_width + columns]  9.36 us
  transfers between devices with their start and end apart: 7, of which 4 were waited for; matrix products, arithmetic and copies ran while one was open for 12% of the time, Pallas kernels for 0%

commit v1 on v0

v1 whole, which is shorter than its diff:
```python
import jax
import jax.numpy as jnp
from jax import lax
from jax.experimental import pallas as pl
from jax.experimental.pallas import tpu as pltpu
from jax.sharding import PartitionSpec as P

COLS = 4096
KSIZE = 21
READ_ROWS = 64
HALO = 20
EXT = READ_ROWS + 2 * HALO
TILE_ROWS = 2 * EXT * 4
TRASH = 32 * TILE_ROWS
GROUPS = 6
WIDE = 9 * 128
LIST = 4224
UNROLL = 16


def iota(shape, axis):
    return lax.broadcasted_iota(jnp.int32, shape, axis)


def order_slots(message_ref, out_ref):
    t = message_ref[...].T
    live = t[0:32] > 0.0
    r = (t[96:128].astype(jnp.int32) >> 12) & 63
    first = live & (r < HALO)
    final = live & (r >= READ_ROWS - HALO)
    inner = live & (r >= HALO) & (r < READ_ROWS - HALO)
    below = (iota((32, 32), 1) < iota((32, 32), 0)).astype(jnp.bfloat16)
    rank = jnp.zeros((32, 128), jnp.float32)
    offset = jnp.zeros((1, 128), jnp.float32)
    for member in (first, inner, final, jnp.logical_not(live)):
        ones = jnp.where(member, 1.0, 0.0)
        before = jnp.dot(below, ones.astype(jnp.bfloat16), preferred_element_type=jnp.float32)
        rank = jnp.where(member, before + offset, rank)
        offset = offset + jnp.sum(ones, axis=0, keepdims=True)
    rank = rank.astype(jnp.int32)
    place = iota((32, 128), 0)
    parts = [jnp.zeros((32, 128), jnp.float32)] * 4
    for s in range(32):
        here = place == rank[s : s + 1]
        parts = [p + jnp.where(here, t[c * 32 + s : c * 32 + s + 1], 0.0) for c, p in enumerate(parts)]
    out_ref[...] = jnp.concatenate(parts, axis=0).T


def tables(band_ref, base1_ref, base2_ref, cross_ref, w1_ref, w2_ref, mix_ref):
    band = band_ref[0]
    row8 = iota((8, 128), 0)
    for half in range(2):
        for c1 in range(GROUPS):
            for q in range(6):
                base = jnp.broadcast_to(base1_ref[half, c1 * 6 + q : c1 * 6 + q + 1, :], (8, 128))
                for blk in range(2):
                    rows = []
                    for g in range(6):
                        start = 2 + g * 8 if blk else (10 + g * 8 if g < 4 else (g - 4) * 8)
                        turned = pltpu.roll(base, start, axis=1, stride=1, stride_axis=0)
                        if g == 5:
                            turned = jnp.where(row8 < 2, turned, 0.0)
                        if blk == 0 and g >= 4:
                            turned = jnp.where(band == 0, 0.0, turned)
                        rows.append(turned)
                    w1_ref[half, blk, c1 * 48 : c1 * 48 + 48, q * 128 : q * 128 + 128] = jnp.concatenate(
                        rows, axis=0
                    ).astype(jnp.bfloat16)
            y = iota((8, 128), 1) & 63
            for q in range(2):
                base = jnp.broadcast_to(base2_ref[half, c1 * 2 + q : c1 * 2 + q + 1, :], (8, 128))
                first, second = [], []
                for g in range(4):

                    def turn(by, g=g, base=base):
                        return pltpu.roll(pltpu.roll(base, by, axis=1), g * 8, axis=1, stride=1, stride_axis=0)

                    late = turn(6)
                    second.append(late)
                    first.append(jnp.where(y < 32, turn(118), jnp.where(y < 48, turn(32), late)))
                for blk, rows in ((0, first), (1, second)):
                    w2_ref[half, blk, c1 * 32 : c1 * 32 + 32, q * 128 : q * 128 + 128] = jnp.concatenate(
                        rows, axis=0
                    ).astype(jnp.bfloat16)
    row = iota((256, 128), 0)
    source = iota((256, 128), 1)
    pick = (((row >> 5) * 16 + (row & 15)) == source).astype(jnp.bfloat16)
    column = iota((16, 256), 1)
    amp = ((column >> 2) & 1) * 8 + (column & 3) * 2 + (column >> 7)
    spread = (iota((16, 256), 0) == amp).astype(jnp.bfloat16)
    row = iota((256, 256), 0)
    column = iota((256, 256), 1)
    same = (row >> 4) == ((column >> 3) & 15)
    for g in range(4):
        wide = jnp.dot(
            cross_ref[g * 128 : g * 128 + 128, :], spread, preferred_element_type=jnp.float32
        ).astype(jnp.bfloat16)
        tall = jnp.dot(pick, wide, preferred_element_type=jnp.float32)
        mix_ref[g] = jnp.where(same, tall, 0.0).astype(jnp.bfloat16)


def shifted(tiles, by):
    if by == 0:
        return tiles
    lane = lax.broadcasted_iota(jnp.int32, tiles[0].shape, 1)
    zero = jnp.zeros_like(tiles[0])
    turned = [pltpu.roll(t, (-by) % 128, axis=1) for t in tiles]
    count = len(tiles)
    if by > 0:
        return [
            jnp.where(lane < 128 - by, turned[m], turned[m + 1] if m + 1 < count else zero)
            for m in range(count)
        ]
    return [jnp.where(lane < -by, turned[m - 1] if m else zero, turned[m]) for m in range(count)]


def photons_to_readout(
    band_ref, list_ref, w1_ref, w2_ref, out_ref,
    acc, turned, key_v, key_s, flat, bext, part, dif, fin, sem,
):
    band = band_ref[0]
    for q in range(3):
        t = list_ref[q].T
        turned[q, 0:128, :] = t
        turned[q, 128:256, :] = t
        live = t[0:32] > 0.0
        pixel = t[96:128].astype(jnp.int32)
        u = pixel >> 12
        x = pixel & 4095
        half = u >> 6
        r = u & 63
        tile = (x & 3) * 8 + (x >> 9)
        lane = (x >> 2) & 127
        total = jnp.sum(jnp.where(live, 1, 0), axis=0, keepdims=True)
        heads = jnp.sum(jnp.where(live & (r < HALO), 1, 0), axis=0, keepdims=True)
        tails = jnp.sum(jnp.where(live & (r >= 44), 1, 0), axis=0, keepdims=True)
        last = band == 3
        if q == 0:
            row, first, many = r + HALO, jnp.zeros_like(total), total
        elif q == 1:
            row, first, many = r - 44, total - tails, tails
        else:
            row = jnp.where(last, 147 - r, 84 + r)
            half = jnp.where(last, 1 - half, half)
            first = jnp.where(last, total - tails, 0)
            many = jnp.where(last, tails, heads)
        e = half * EXT + row
        slot = iota((32, 128), 0)
        rot = (lane - iota((32, 128), 1)) & 127
        key_v[q, 0:32, :] = ((tile * EXT + (e >> 1)) << 20) + (((e & 1) * 128 + lane) << 12) + (rot << 5) + slot
        key_v[q, 32:40, :] = jnp.broadcast_to(first, (8, 128))
        key_v[q, 40:48, :] = jnp.broadcast_to(many, (8, 128))
    copy = pltpu.make_async_copy(key_v, key_s, sem)
    copy.start()

    def clear(i, c):
        acc[pl.ds(pl.multiple_of(i * 512, 512), 512), :] = jnp.zeros((512, 128), jnp.float32)
        return c

    lax.fori_loop(0, TRASH // 512, clear, 0)
    acc[TRASH : TRASH + 8, :] = jnp.zeros((8, 128), jnp.float32)
    copy.wait()
    spot = iota((8, 128), 1) + 128 * (iota((8, 128), 0) >> 2)
    for q in range(3):
        step = 8 if q == 0 else 4

        def sender(i, at, q=q, step=step):
            first = key_s[q, 32, i]
            many = key_s[q, 40, i]

            def some(j, c):
                for v in range(step):
                    flat[at + j * step + v] = key_s[q, first + j * step + v, i]
                return c

            some(0, 0)
            lax.fori_loop(1, (many + step - 1) // step, some, 0)
            return at + many

        size = lax.fori_loop(0, 128, sender, 0)

        def finish(i, c, size=size):
            flat[size + i] = jnp.int32(((TRASH // 8) << 20) - (1 << 32))
            return c

        lax.fori_loop(0, 2 * UNROLL, finish, 0)

        def prepare(j, q=q):
            bases, values = [], []
            for v in range(UNROLL):
                key = flat[j * UNROLL + v]
                bases.append(pl.multiple_of(lax.shift_right_logical(key, 20) * 8, 8))
                target = lax.shift_right_logical(key, 12) & 255
                charges = turned[q, pl.ds(key & 31, 8, stride=32), :]
                moved = pltpu.roll(charges, (key >> 5) & 127, axis=1)
                values.append(jnp.where(spot == target, moved, 0.0))
            return tuple(bases), tuple(values)

        def add(j, carry, prepare=prepare):
            bases, values = carry
            following = prepare(j + 1)
            for base, value in zip(bases, values):
                acc[pl.ds(pl.multiple_of(base, 8), 8), :] += value
            return following

        lax.fori_loop(0, (size + UNROLL - 1) // UNROLL, add, prepare(0))

    def diffuse(which, carry):
        half = which >> 1
        blk = which & 1
        start = (half * EXT + blk * 40) * 4
        pad = [jnp.zeros((64, 128), jnp.float32)]
        for p in range(4):
            for k in range(3):
                tiles = pad + [
                    acc[pl.ds((p * 8 + m) * TILE_ROWS + start + k, 64, stride=4), :] for m in range(8)
                ]

                def put(slot, values, k=k):
                    for m in range(9):
                        bext[slot * 192 + k * 64 : slot * 192 + k * 64 + 64, m * 128 : m * 128 + 128] = (
                            values[m].astype(jnp.bfloat16)
                        )

                if p >= 2:
                    put(p - 2, tiles)
                put(p + 2, shifted(tiles, 1))
                if p == 0:
                    put(6, shifted(tiles, 2))
        for t in range(4):
            part[...] = jnp.dot(
                w1_ref[half, blk], bext[t * 192 : (t + 4) * 192, :], preferred_element_type=jnp.float32
            )
            for g in range(3):
                total = gathered(part, 48, g)
                rounded = [jnp.zeros((16, 128), jnp.float32)] + [
                    v.astype(jnp.bfloat16).astype(jnp.float32) for v in total
                ]
                row = pl.multiple_of(blk * 48 + g * 16, 16)

                def keep(slot, values, row=row):
                    for m in range(9):
                        dif[half, slot, pl.ds(row, 16), m * 128 : m * 128 + 128] = values[m].astype(jnp.bfloat16)

                keep(t - 2 if t >= 2 else t + 7, rounded)
                keep(t + 2, shifted(rounded, 1))
                if t == 0:
                    keep(6, shifted(rounded, 2))
        return carry

    lax.fori_loop(0, 4, diffuse, 0)

    def respond(half, carry):
        for blk in range(2):
            for t in range(4):
                pieces = []
                for slot in range(t, t + 4):
                    if blk == 0:
                        pieces.append(dif[half, slot, 0:64, :])
                    else:
                        pieces.append(dif[half, slot, 16:32, :])
                        pieces.append(dif[half, slot, 48:96, :])
                part[0:192, :] = jnp.dot(
                    w2_ref[half, blk], jnp.concatenate(pieces, axis=0), preferred_element_type=jnp.float32
                )
                natural = t - 2 if t >= 2 else t + 7
                for g in range(2):
                    total = gathered(part, 32, g)
                    row = blk * 48 + g * 16
                    for m in range(8):
                        d = dif[half, natural, row : row + 16, m * 128 + 128 : m * 128 + 256].astype(jnp.float32)
                        final = d * (1.0 - total[m])
                        for o in range(2):
                            r0 = blk * 32 + g * 16 + o * 8
                            fin[t, pl.ds(r0 * 16 + (m % 2) * 8 + half * 4 + m // 2, 8, stride=16), :] = final[
                                o * 8 : o * 8 + 8
                            ]
        return carry

    lax.fori_loop(0, 2, respond, 0)

    def pack(d, c):
        base = pl.multiple_of(d * 32, 32)
        for t in range(4):
            a = fin[t, pl.ds(base, 32), :]
            swapped = jnp.concatenate([a[0:8], a[16:24], a[8:16], a[24:32]], axis=0)
            out_ref[d, :, t * 128 : t * 128 + 128] = swapped.astype(jnp.bfloat16)
        return c

    lax.fori_loop(0, 32, pack, 0)


def gathered(part, size, g):
    total = None
    for c1 in range(GROUPS):
        rows = c1 * size + g * 16
        tiles = shifted([part[rows : rows + 16, m * 128 : m * 128 + 128] for m in range(9)], c1 - 3)[1:]
        total = tiles if total is None else [a + b for a, b in zip(total, tiles)]
    return total


def crosstalk_kernel(got_ref, mix_ref, out_ref):
    source = lax.broadcasted_iota(jnp.int32, (512, 512), 0)
    column = lax.broadcasted_iota(jnp.int32, (512, 512), 1)
    place = (source & 127) * 4 + (source >> 7)
    even = (place == column).astype(jnp.bfloat16)
    odd = (511 - place == column).astype(jnp.bfloat16)
    for g in range(4):
        block = got_ref[g * 8 : g * 8 + 8]
        ordered = []
        for parity, order in ((0, even), (1, odd)):
            rows = block[:, parity * 16 : parity * 16 + 16, :].reshape(128, 512)
            ordered.append(jnp.dot(rows, order, preferred_element_type=jnp.float32).astype(jnp.bfloat16))
        mixed = jnp.dot(
            mix_ref[g], jnp.concatenate(ordered, axis=0), preferred_element_type=jnp.float32
        )
        for s in range(8):
            for r in range(2):
                for i0 in range(0, 16, 8):
                    for m in range(4):
                        row = s * 32 + r * 16 + i0
                        start = ((g * 8 + s) * 16 + i0) * 8 + m * 2 + r
                        out_ref[pl.ds(start, 8, stride=8), :] = mixed[row : row + 8, m * 128 : m * 128 + 128]


def shards(photon_charge, photon_pixel, photon_count, diffusion_kernel, fatter_kernel, crosstalk):
    vmem = pl.BlockSpec(memory_space=pltpu.VMEM)
    smem = pl.BlockSpec(memory_space=pltpu.SMEM)
    limit = pltpu.CompilerParams(vmem_limit_bytes=56 * 1024 * 1024)
    counts = photon_count[0]
    live = jnp.arange(32, dtype=jnp.int32)[None, :] < counts[:, None]
    charge = jnp.where(live[:, None, :], photon_charge[0], jnp.zeros((), jnp.bfloat16))
    message = jnp.concatenate(
        [charge.reshape(128, 96).astype(jnp.float32), photon_pixel[0].astype(jnp.float32)], axis=1
    )
    message = pl.pallas_call(
        order_slots,
        out_shape=jax.ShapeDtypeStruct((128, 128), jnp.float32),
        in_specs=[vmem],
        out_specs=vmem,
    )(message)
    own = lax.all_to_all(message, ("sensor", "rows"), split_axis=0, concat_axis=0, tiled=True)
    band = lax.axis_index("rows")

    dk = jnp.pad(diffusion_kernel.astype(jnp.float32), ((0, 0), (0, 43), (0, 3)))
    dk = jnp.stack([dk, jnp.pad(jnp.flip(dk[:, :KSIZE], axis=1), ((0, 0), (0, 43), (0, 0)))])
    base1 = jnp.transpose(dk, (0, 3, 1, 2)).reshape(2, 36, 128)
    fk = jnp.pad(fatter_kernel.astype(jnp.float32), ((0, 43), (0, 3)))
    fk = jnp.stack([fk, jnp.pad(jnp.flip(fk[:KSIZE], axis=0), ((0, 43), (0, 0)))])
    base2 = jnp.transpose(fk, (0, 2, 1)).reshape(2, 12, 128)
    w1, w2, mix = pl.pallas_call(
        tables,
        out_shape=[
            jax.ShapeDtypeStruct((2, 2, 288, 768), jnp.bfloat16),
            jax.ShapeDtypeStruct((2, 2, 192, 256), jnp.bfloat16),
            jax.ShapeDtypeStruct((4, 256, 256), jnp.bfloat16),
        ],
        in_specs=[smem, vmem, vmem, vmem],
        out_specs=[vmem, vmem, vmem],
        cost_estimate=pl.CostEstimate(flops=10**8, bytes_accessed=4 * 10**6, transcendentals=0),
    )(band.reshape(1), base1, base2, crosstalk.reshape(512, 16))

    low = lax.ppermute(own, "rows", [(0, 1), (1, 2), (2, 3)])
    high = lax.ppermute(own, "rows", [(1, 0), (2, 1), (3, 2)])
    high = jnp.where(band == 3, own, high)
    lists = jnp.stack([own, low, high])
    amplifiers = pl.pallas_call(
        photons_to_readout,
        out_shape=jax.ShapeDtypeStruct((32, 32, 512), jnp.bfloat16),
        in_specs=[smem, vmem, vmem, vmem],
        out_specs=vmem,
        scratch_shapes=[
            pltpu.VMEM((TRASH + 8, 128), jnp.float32),
            pltpu.VMEM((3, 256, 128), jnp.float32),
            pltpu.VMEM((3, 48, 128), jnp.int32),
            pltpu.SMEM((3, 48, 128), jnp.int32),
            pltpu.SMEM((LIST,), jnp.int32),
            pltpu.VMEM((7 * 192, WIDE), jnp.bfloat16),
            pltpu.VMEM((288, WIDE), jnp.float32),
            pltpu.VMEM((2, 9, 96, WIDE), jnp.bfloat16),
            pltpu.VMEM((4, 1024, 128), jnp.float32),
            pltpu.SemaphoreType.DMA,
        ],
        compiler_params=limit,
    )(band.reshape(1), lists, w1, w2)

    got = lax.all_to_all(amplifiers, "sensor", split_axis=0, concat_axis=0, tiled=True)
    flat = pl.pallas_call(
        crosstalk_kernel,
        out_shape=jax.ShapeDtypeStruct((4096, 128), jnp.float32),
        in_specs=[vmem, vmem],
        out_specs=vmem,
    )(got, mix)
    flat = flat.reshape(32, 16, 4, 2, 128)
    return jnp.transpose(flat, (0, 1, 3, 2, 4)).reshape(32, 16, 1, 2, 512)


def solution(mesh):
    placed = (
        P(("sensor", "rows"), None, None, None),
        P(("sensor", "rows"), None, None),
        P(("sensor", "rows"), None),
        P(),
        P(),
        P(),
    )
    return jax.shard_map(
        shards,
        mesh=mesh,
        in_specs=placed,
        out_specs=P(None, None, "rows", "sensor", None),
        check_vma=False,
    )
```

time: 365 us -> 132 us (0.36)
  matrix products: 191 us -> 0 us
  local copies, waits for them, and re-layouts: 70.5 us -> 6.62 us
  Pallas kernels: 0 us -> 60.1 us
  blocking collectives: 0 us -> 38.8 us
  other arithmetic: 31.4 us -> 2.13 us
  waiting for transfers between devices: 35.5 us -> 10 us
  starting transfers between devices: 31.9 us -> 14 us
    dot_general x49 -> x0, matrix products: 191 us -> none  [the longest x42 157 us: add_row(): jnp.einsum('chrnw,hcwo->hrno', row_slab, matrix, preferred_element_type=j...]
    pallas_call x0 -> x4, Pallas kernels: none -> 60.1 us  [the longest x1 49.9 us: shards(): pl.pallas_call(photons_to_readout, out_shape=jax.ShapeDtypeStruct((32, 32...]
    all_to_all x0 -> x1, blocking collectives: none -> 38.8 us  [shards(): lax.all_to_all(amplifiers, 'sensor', split_axis=0, concat_axis=0, tiled=T...]
    rev x5 -> x2, local copies, waits for them, and re-layouts: 26.4 us -> 0.15 us  [the longest x1 0.07 us: shards(): jnp.flip(fk[:KSIZE], axis=0)]
    all_to_all x3 -> x1, waiting for transfers between devices: 29.6 us -> 6.35 us  [shards(): lax.all_to_all(message, ('sensor', 'rows'), split_axis=0, concat_axis=0,...]
    reshape x7 -> x2, local copies, waits for them, and re-layouts: 20.8 us -> 1.37 us  [the longest x1 0.71 us: shards(): base1 = jnp.transpose(dk, (0, 3, 1, 2)).reshape(2, 36, 128)]
    concatenate x4 -> x1, other arithmetic: 17.8 us -> 0.72 us  [shards(): jnp.concatenate([charge.reshape(128, 96).astype(jnp.float32), photon_pixe...]
    all_to_all x3 -> x1, starting transfers between devices: 22.5 us -> 10.8 us  [shards(): lax.all_to_all(message, ('sensor', 'rows'), split_axis=0, concat_axis=0,...]
  transfers between devices with their start and end apart: 7 -> 3, of which waited for: 4 -> 2; matrix products, arithmetic and copies ran while one was open for 12% -> 4% of each run, Pallas kernels for 0% -> 3%
where the time goes in v1:
time: 132 us
  Pallas kernels  60.1 us (46%)
  blocking collectives  38.8 us (29%)
  starting transfers between devices  14 us (11%)
  waiting for transfers between devices  10 us (8%)
  local copies, waits for them, and re-layouts  6.62 us (5%)
  other arithmetic  2.13 us (2%)
    pallas_call x1, Pallas kernels, shards(): pl.pallas_call(photons_to_readout, out_shape=jax.ShapeDtypeStruct((32, 32...  49.9 us
    all_to_all x1, blocking collectives, shards(): lax.all_to_all(amplifiers, 'sensor', split_axis=0, concat_axis=0, tiled=T...  38.8 us
    all_to_all x1, starting transfers between devices, shards(): lax.all_to_all(message, ('sensor', 'rows'), split_axis=0, concat_axis=0,...  10.8 us
    all_to_all x1, waiting for transfers between devices, shards(): lax.all_to_all(message, ('sensor', 'rows'), split_axis=0, concat_axis=0,...  6.35 us
    pallas_call x1, Pallas kernels, shards(): pl.pallas_call(crosstalk_kernel, out_shape=jax.ShapeDtypeStruct((4096, 12...  4.37 us
    unnamed x4, local copies, waits for them, and re-layouts  4.09 us
    pallas_call x1, Pallas kernels, shards(): pl.pallas_call(tables, out_shape=[jax.ShapeDtypeStruct((2, 2, 288, 768),...  3.79 us
    ppermute x1, waiting for transfers between devices, shards(): low = lax.ppermute(own, 'rows', [(0, 1), (1, 2), (2, 3)])  3.68 us
  transfers between devices with their start and end apart: 3, of which 2 were waited for; matrix products, arithmetic and copies ran while one was open for 4% of the time, Pallas kernels for 3%

profile of v1, /device:TPU:7, one launch (start us, length us, event | category | flops | bytes accessed | tf_op | source)
XLA Modules:
  0.0 131.8 jit_solution(17913266895694147512)
XLA Ops:
  0.0 0.7 iota_compare_fusion
  0.7 0.1 copy.20
  0.8 0.8 copy.21
  1.6 0.8 copy.22
  2.5 0.7 pad_maximum_fusion.1.message_ref
  3.2 2.0 %shard_map.64 = f32[128,128]{1,0:T(8,128)} custom-call(f32[128,128]{1,0:T(8,128)} %pad_maximum_fusion.1.message_ref), custom_call_target="tpu_custom_call" | custom-call | tf_op jit(solution)/shard_map/pallas_call | solution.py:336
  5.2 10.8 %all-to-all-start = ((f32[128,1,128]{2,1,0:T(1,128)}), f32[128,1,128]{2,1,0:T(1,128)S(1)}, u32[]{:S(2)}, u32[]{:S(2)}) async-start(f32[128,1,128]{2,1,0:T(1,128)} %bitcast.38), calls=%async_computation | async-start | bytes 131072 | tf_op jit(solution)/shard_map/all_to_all | solution.py:342
  16.0 0.8 copy.26
  16.8 0.8 copy.24
  17.6 0.1 rev.9
  17.7 0.1 rev.8
  17.8 6.4 %all-to-all-done = f32[128,1,128]{2,1,0:T(1,128)S(1)} async-done(((f32[128,1,128]{2,1,0:T(1,128)}), f32[128,1,128]{2,1,0:T(1,128)S(1)}, u32[]{:S(2)}, u32[]{:S(2)}) %all-to-all-start) | async-done | bytes 65568 | tf_op jit(solution)/shard_map/all_to_all | solution.py:342
  24.2 2.0 %collective-permute-start.1 = (f32[128,128]{1,0:T(8,128)S(1)}, f32[128,128]{1,0:T(8,128)S(1)}, u32[]{:S(2)}, u32[]{:S(2)}) collective-permute-start(f32[128,128]{1,0:T(8,128)S(1)} %bitcast.34), channel_id=1, source_target_pairs={{1,0},{2,1},{3,2},{5,4},{6,5},{7,6},{9,8},{10,9},{11,10},{13,12},{... | collective-permute-start | bytes 196616 | tf_op jit(solution)/shard_map/ppermute | solution.py:364
  26.2 0.7 reshape.48.base2_ref
  26.9 0.7 reshape.47.base1_ref
  27.6 1.6 %copy.27 = bf16[32,16,16]{2,1,0:T(8,128)(2,1)} copy(bf16[32,16,16]{0,2,1:T(8,128)(2,1)} %param.11) | data formatting | bytes 32768 | tf_op args[5]
  29.2 3.8 %shard_map.65 = (bf16[2,2,288,768]{3,2,1,0:T(8,128)(2,1)}, bf16[2,2,192,256]{3,2,1,0:T(8,128)(2,1)}, bf16[4,256,256]{2,1,0:T(8,128)(2,1)}) custom-call(s32[1]{0:T(128)} %bitcast.band_ref, f32[2,36,128]{2,1,0:T(8,128)} %reshape.47.base1_ref, f32[2,12,128]{2,1,0:T(8,128)} %reshape.48.base2_ref, bf16[512,16]{1,0:T(8,128)(2,1)} %bitcast.40), custom_call_target="tpu_custom_call" | custom-call | flops 100000000 | bytes 4000000 | tf_op jit(solution)/shard_map/pallas_call | solution.py:351
  33.0 1.3 collective-permute-start
  34.3 0.0 collective-permute-done.1
  34.3 3.7 %collective-permute-done = f32[128,128]{1,0:T(8,128)S(1)} collective-permute-done((f32[128,128]{1,0:T(8,128)S(1)}, f32[128,128]{1,0:T(8,128)S(1)}, u32[]{:S(2)}, u32[]{:S(2)}) %collective-permute-start) | collective-permute-done | bytes 65568 | tf_op jit(solution)/shard_map/ppermute | solution.py:363
  38.0 0.7 pad_maximum_fusion.list_ref
  38.7 49.9 %shard_map.66 = bf16[32,32,512]{2,1,0:T(8,128)(2,1)} custom-call(s32[1]{0:T(128)} %bitcast.band_ref, f32[3,128,128]{2,1,0:T(8,128)} %pad_maximum_fusion.list_ref, bf16[2,2,288,768]{3,2,1,0:T(8,128)(2,1)} %get-tuple-element.8.w1_ref, bf16[2,2,192,256]{3,2,1,0:T(8,128)(2,1)} %get-tuple-element.9.w2_ref), custom_call_target="tpu_custom_call" | custom-call | tf_op jit(solution)/shard_map/pallas_call | solution.py:367
  88.6 38.8 %all_to_all.17.got_ref = bf16[32,32,512]{2,1,0:T(8,128)(2,1)} all-to-all(bf16[32,32,512]{2,1,0:T(8,128)(2,1)} %shard_map.66), channel_id=1, replica_groups=mesh['sensor'=32,'rows'=4] {'sensor'}, dimensions={0} | all-to-all | bytes 2097152 | tf_op jit(solution)/shard_map/all_to_all | solution.py:387
  127.4 4.4 %shard_map.67 = f32[4096,128]{1,0:T(8,128)} custom-call(bf16[32,32,512]{2,1,0:T(8,128)(2,1)} %all_to_all.17.got_ref, bf16[4,256,256]{2,1,0:T(8,128)(2,1)} %get-tuple-element.10.mix_ref), custom_call_target="tpu_custom_call" | custom-call | tf_op jit(solution)/shard_map/pallas_call | solution.py:388
  (11 shorter events, 0.1 us)
Async XLA Ops:
  5.2 19.0 %all-to-all-start = ((f32[128,1,128]{2,1,0:T(1,128)}), f32[128,1,128]{2,1,0:T(1,128)S(1)}, u32[]{:S(2)}, u32[]{:S(2)}) async-start(f32[128,1,128]{2,1,0:T(1,128)} %bitcast.38), calls=%async_computation | async-start | bytes 131072 | tf_op jit(solution)/shard_map/all_to_all | solution.py:342
  24.2 10.1 %collective-permute-start.1 = (f32[128,128]{1,0:T(8,128)S(1)}, f32[128,128]{1,0:T(8,128)S(1)}, u32[]{:S(2)}, u32[]{:S(2)}) collective-permute-start(f32[128,128]{1,0:T(8,128)S(1)} %bitcast.34), channel_id=1, source_target_pairs={{1,0},{2,1},{3,2},{5,4},{6,5},{7,6},{9,8},{10,9},{11,10},{13,12},{... | collective-permute-start | bytes 196616 | tf_op jit(solution)/shard_map/ppermute | solution.py:364
  33.0 5.0 %collective-permute-start = (f32[128,128]{1,0:T(8,128)S(1)}, f32[128,128]{1,0:T(8,128)S(1)}, u32[]{:S(2)}, u32[]{:S(2)}) collective-permute-start(f32[128,128]{1,0:T(8,128)S(1)} %bitcast.35), channel_id=1, source_target_pairs={{0,1},{1,2},{2,3},{4,5},{5,6},{6,7},{8,9},{9,10},{10,11},{12,13},{... | collective-permute-start | bytes 196616 | tf_op jit(solution)/shard_map/ppermute | solution.py:363

commit v2 on v1

--- a/solution.py
+++ b/solution.py
@@ -120,7 +120,12 @@
 ):
     band = band_ref[0]
     for q in range(3):
-        t = list_ref[q].T
+        t = list_ref[q]
+        if q == 1:
+            t = jnp.where(band == 0, 0.0, t)
+        if q == 2:
+            t = jnp.where(band == 3, list_ref[0], t)
+        t = t.T
         turned[q, 0:128, :] = t
         turned[q, 128:256, :] = t
         live = t[0:32] > 0.0
@@ -299,6 +304,105 @@
     return total
 
 
+def exchange_photons(message_ref, out_ref, send_sem, recv_sem, own_sem, side_sem):
+    sensor = lax.axis_index("sensor")
+    band = lax.axis_index("rows")
+    me = sensor * 4 + band
+    barrier = pltpu.get_barrier_semaphore()
+
+    def greet(k, c):
+        peer = lax.rem(me + k, 128)
+        pl.semaphore_signal(
+            barrier, inc=1, device_id=(peer // 4, lax.rem(peer, 4)), device_id_type=pl.DeviceIdType.MESH
+        )
+        return c
+
+    lax.fori_loop(1, 128, greet, 0)
+    pl.semaphore_wait(barrier, 127)
+    own = pltpu.make_async_copy(message_ref.at[me], out_ref.at[0, me], own_sem)
+    own.start()
+
+    def send(k, c):
+        peer = lax.rem(me + k, 128)
+        pltpu.make_async_remote_copy(
+            src_ref=message_ref.at[peer],
+            dst_ref=out_ref.at[0, me],
+            send_sem=send_sem,
+            recv_sem=recv_sem,
+            device_id=(peer // 4, lax.rem(peer, 4)),
+            device_id_type=pl.DeviceIdType.MESH,
+        ).start()
+        return c
+
+    lax.fori_loop(1, 128, send, 0)
+    own.wait()
+    everything = pltpu.make_async_remote_copy(
+        src_ref=message_ref.at[pl.ds(0, 127)],
+        dst_ref=out_ref.at[0, pl.ds(0, 127)],
+        send_sem=send_sem,
+        recv_sem=recv_sem,
+        device_id=(sensor, lax.rem(band + 1, 4)),
+        device_id_type=pl.DeviceIdType.MESH,
+    )
+    everything.wait_recv()
+    copies = []
+    for side, to in ((1, 1), (2, 3)):
+        copy = pltpu.make_async_remote_copy(
+            src_ref=out_ref.at[0],
+            dst_ref=out_ref.at[side],
+            send_sem=side_sem.at[side - 1],
+            recv_sem=side_sem.at[side + 1],
+            device_id=(sensor, lax.rem(band + to, 4)),
+            device_id_type=pl.DeviceIdType.MESH,
+        )
+        copy.start()
+        copies.append(copy)
+    everything.wait_send()
+    for copy in copies:
+        copy.wait()
+
+
+def exchange_readout(block_ref, out_ref, send_sem, recv_sem, own_sem):
+    me = lax.axis_index("sensor")
+    band = lax.axis_index("rows")
+    barrier = pltpu.get_barrier_semaphore()
+
+    def greet(k, c):
+        pl.semaphore_signal(
+            barrier, inc=1, device_id=(lax.rem(me + k, 32), band), device_id_type=pl.DeviceIdType.MESH
+        )
+        return c
+
+    lax.fori_loop(1, 32, greet, 0)
+    pl.semaphore_wait(barrier, 31)
+    own = pltpu.make_async_copy(block_ref.at[me], out_ref.at[me], own_sem)
+    own.start()
+
+    def send(k, c):
+        peer = lax.rem(me + k, 32)
+        pltpu.make_async_remote_copy(
+            src_ref=block_ref.at[peer],
+            dst_ref=out_ref.at[me],
+            send_sem=send_sem,
+            recv_sem=recv_sem,
+            device_id=(peer, band),
+            device_id_type=pl.DeviceIdType.MESH,
+        ).start()
+        return c
+
+    lax.fori_loop(1, 32, send, 0)
+    own.wait()
+    everything = pltpu.make_async_remote_copy(
+        src_ref=block_ref.at[pl.ds(0, 31)],
+        dst_ref=out_ref.at[pl.ds(0, 31)],
+        send_sem=send_sem,
+        recv_sem=recv_sem,
+        device_id=(lax.rem(me + 1, 32), band),
+        device_id_type=pl.DeviceIdType.MESH,
+    )
+    everything.wait()
+
+
 def crosstalk_kernel(got_ref, mix_ref, out_ref):
     source = lax.broadcasted_iota(jnp.int32, (512, 512), 0)
     column = lax.broadcasted_iota(jnp.int32, (512, 512), 1)
@@ -339,7 +443,19 @@
         in_specs=[vmem],
         out_specs=vmem,
     )(message)
-    own = lax.all_to_all(message, ("sensor", "rows"), split_axis=0, concat_axis=0, tiled=True)
+    lists = pl.pallas_call(
+        exchange_photons,
+        out_shape=jax.ShapeDtypeStruct((3, 128, 1, 128), jnp.float32),
+        in_specs=[vmem],
+        out_specs=vmem,
+        scratch_shapes=[
+            pltpu.SemaphoreType.DMA,
+            pltpu.SemaphoreType.DMA,
+            pltpu.SemaphoreType.DMA,
+            pltpu.SemaphoreType.DMA((4,)),
+        ],
+        compiler_params=pltpu.CompilerParams(collective_id=0, has_side_effects=True),
+    )(message.reshape(128, 1, 128)).reshape(3, 128, 128)
     band = lax.axis_index("rows")
 
     dk = jnp.pad(diffusion_kernel.astype(jnp.float32), ((0, 0), (0, 43), (0, 3)))
@@ -360,10 +476,6 @@
         cost_estimate=pl.CostEstimate(flops=10**8, bytes_accessed=4 * 10**6, transcendentals=0),
     )(band.reshape(1), base1, base2, crosstalk.reshape(512, 16))
 
-    low = lax.ppermute(own, "rows", [(0, 1), (1, 2), (2, 3)])
-    high = lax.ppermute(own, "rows", [(1, 0), (2, 1), (3, 2)])
-    high = jnp.where(band == 3, own, high)
-    lists = jnp.stack([own, low, high])
     amplifiers = pl.pallas_call(
         photons_to_readout,
         out_shape=jax.ShapeDtypeStruct((32, 32, 512), jnp.bfloat16),
@@ -384,7 +496,14 @@
         compiler_params=limit,
     )(band.reshape(1), lists, w1, w2)
 
-    got = lax.all_to_all(amplifiers, "sensor", split_axis=0, concat_axis=0, tiled=True)
+    got = pl.pallas_call(
+        exchange_readout,
+        out_shape=jax.ShapeDtypeStruct((32, 32, 512), jnp.bfloat16),
+        in_specs=[vmem],
+        out_specs=vmem,
+        scratch_shapes=[pltpu.SemaphoreType.DMA, pltpu.SemaphoreType.DMA, pltpu.SemaphoreType.DMA],
+        compiler_params=pltpu.CompilerParams(collective_id=1, has_side_effects=True),
+    )(amplifiers)
     flat = pl.pallas_call(
         crosstalk_kernel,
         out_shape=jax.ShapeDtypeStruct((4096, 128), jnp.float32),

time: 132 us -> 125 us (0.947)
  Pallas kernels: 60.1 us -> 116 us
  blocking collectives: 38.8 us -> 0 us
  starting transfers between devices: 14 us -> 0 us
  waiting for transfers between devices: 10 us -> 0 us
    pallas_call x0 -> x2, Pallas kernels: none -> 54.6 us  [the longest x1 35.5 us: shards(): pl.pallas_call(exchange_readout, out_shape=jax.ShapeDtypeStruct((32, 32,...]
    all_to_all x1 -> x0, blocking collectives: 38.8 us -> none  [shards(): lax.all_to_all(amplifiers, 'sensor', split_axis=0, concat_axis=0, tiled=T...]
    all_to_all x1 -> x0, starting transfers between devices: 10.8 us -> none  [shards(): lax.all_to_all(message, ('sensor', 'rows'), split_axis=0, concat_axis=0,...]
    all_to_all x1 -> x0, waiting for transfers between devices: 6.35 us -> none  [shards(): lax.all_to_all(message, ('sensor', 'rows'), split_axis=0, concat_axis=0,...]
    ppermute x2 -> x0, waiting for transfers between devices: 3.68 us -> none  [the longest x1 3.68 us: shards(): low = lax.ppermute(own, 'rows', [(0, 1), (1, 2), (2, 3)])]
    ppermute x2 -> x0, starting transfers between devices: 3.24 us -> none  [the longest x1 1.96 us: shards(): high = lax.ppermute(own, 'rows', [(1, 0), (2, 1), (3, 2)])]
  transfers between devices with their start and end apart: 3 -> 0, of which waited for: 2 -> 0; matrix products, arithmetic and copies ran while one was open for 4% -> 0% of each run, Pallas kernels for 3% -> 0%
where the time goes in v2:
time: 125 us; the launch traced here: 124 us
  Pallas kernels  116 us (93%)
  local copies, waits for them, and re-layouts  6.63 us (5%)
  other arithmetic  1.43 us (1%)
    pallas_call x1, Pallas kernels, shards(): pl.pallas_call(photons_to_readout, out_shape=jax.ShapeDtypeStruct((32, 32...  51.2 us
    pallas_call x1, Pallas kernels, shards(): pl.pallas_call(exchange_readout, out_shape=jax.ShapeDtypeStruct((32, 32,...  35.5 us
    pallas_call x1, Pallas kernels, shards(): pl.pallas_call(exchange_photons, out_shape=jax.ShapeDtypeStruct((3, 128,...  19.2 us
    pallas_call x1, Pallas kernels, shards(): pl.pallas_call(crosstalk_kernel, out_shape=jax.ShapeDtypeStruct((4096, 12...  4.37 us
    unnamed x4, local copies, waits for them, and re-layouts  4.09 us
    pallas_call x1, Pallas kernels, shards(): pl.pallas_call(tables, out_shape=[jax.ShapeDtypeStruct((2, 2, 288, 768),...  3.78 us

profile of v2, /device:TPU:7, one launch (start us, length us, event | category | flops | bytes accessed | tf_op | source)
XLA Modules:
  0.0 124.1 jit_solution(4058747066464246465)
XLA Ops:
  0.0 0.7 iota_compare_fusion
  0.7 0.8 copy.25
  1.5 0.1 copy.20
  1.6 0.8 copy.23
  2.4 0.1 rev.9
  2.5 0.7 reshape.53.base2_ref
  3.2 0.8 copy.21
  4.1 0.1 rev.8
  4.2 0.7 reshape.52.base1_ref
  4.9 0.8 copy.22
  5.8 0.7 pad_maximum_fusion.message_ref
  6.5 2.0 %shard_map.64 = f32[128,128]{1,0:T(8,128)} custom-call(f32[128,128]{1,0:T(8,128)} %pad_maximum_fusion.message_ref), custom_call_target="tpu_custom_call" | custom-call | tf_op jit(solution)/shard_map/pallas_call | solution.py:440
  8.5 19.2 %shard_map.65 = f32[3,128,1,128]{3,2,1,0:T(1,128)} custom-call(f32[128,1,128]{2,1,0:T(1,128)} %bitcast.29), custom_call_target="tpu_custom_call" | custom-call | tf_op jit(solution)/shard_map/pallas_call | solution.py:446
  27.7 1.6 %copy.26 = bf16[32,16,16]{2,1,0:T(8,128)(2,1)} copy(bf16[32,16,16]{0,2,1:T(8,128)(2,1)} %param.11) | data formatting | bytes 32768 | tf_op args[5]
  29.3 3.8 %shard_map.66 = (bf16[2,2,288,768]{3,2,1,0:T(8,128)(2,1)}, bf16[2,2,192,256]{3,2,1,0:T(8,128)(2,1)}, bf16[4,256,256]{2,1,0:T(8,128)(2,1)}) custom-call(s32[1]{0:T(128)} %bitcast.band_ref, f32[2,36,128]{2,1,0:T(8,128)} %reshape.52.base1_ref, f32[2,12,128]{2,1,0:T(8,128)} %reshape.53.base2_ref, bf16[512,16]{1,0:T(8,128)(2,1)} %bitcast.31), custom_call_target="tpu_custom_call" | custom-call | flops 100000000 | bytes 4000000 | tf_op jit(solution)/shard_map/pallas_call | solution.py:467
  33.1 51.2 %shard_map.67.block_ref = bf16[32,32,512]{2,1,0:T(8,128)(2,1)} custom-call(s32[1]{0:T(128)} %bitcast.band_ref, f32[3,128,128]{2,1,0:T(8,128)} %bitcast.28, bf16[2,2,288,768]{3,2,1,0:T(8,128)(2,1)} %get-tuple-element.8.w1_ref, bf16[2,2,192,256]{3,2,1,0:T(8,128)(2,1)} %get-tuple-element.9.w2_ref), custom_call_target="tpu_custom_call" | custom-call | tf_op jit(solution)/shard_map/pallas_call | solution.py:479
  84.3 35.5 %shard_map.68.got_ref = bf16[32,32,512]{2,1,0:T(8,128)(2,1)} custom-call(bf16[32,32,512]{2,1,0:T(8,128)(2,1)} %shard_map.67.block_ref), custom_call_target="tpu_custom_call" | custom-call | tf_op jit(solution)/shard_map/pallas_call | solution.py:499
  119.8 4.4 %shard_map.69 = f32[4096,128]{1,0:T(8,128)} custom-call(bf16[32,32,512]{2,1,0:T(8,128)(2,1)} %shard_map.68.got_ref, bf16[4,256,256]{2,1,0:T(8,128)(2,1)} %get-tuple-element.10.mix_ref), custom_call_target="tpu_custom_call" | custom-call | tf_op jit(solution)/shard_map/pallas_call | solution.py:507
  (10 shorter events, 0.1 us)

commit v3 on v2

--- a/solution.py
+++ b/solution.py
@@ -116,30 +116,28 @@
 
 def photons_to_readout(
     band_ref, list_ref, w1_ref, w2_ref, out_ref,
-    acc, turned, key_v, key_s, flat, bext, part, dif, fin, sem,
+    acc, dense, turned, key_v, key_s, flat0, flat1, flat2, bext, part, dif, fin, sem,
 ):
     band = band_ref[0]
+    last = band == 3
+    spread = iota((128, 128), 1)
     for q in range(3):
         t = list_ref[q]
         if q == 1:
             t = jnp.where(band == 0, 0.0, t)
         if q == 2:
-            t = jnp.where(band == 3, list_ref[0], t)
-        t = t.T
-        turned[q, 0:128, :] = t
-        turned[q, 128:256, :] = t
-        live = t[0:32] > 0.0
-        pixel = t[96:128].astype(jnp.int32)
+            t = jnp.where(last, list_ref[0], t)
+        live = (t > 0.0) & (spread < 32)
+        pixel = pltpu.roll(t, 32, axis=1).astype(jnp.int32) & (2 * READ_ROWS * COLS - 1)
         u = pixel >> 12
         x = pixel & 4095
         half = u >> 6
         r = u & 63
         tile = (x & 3) * 8 + (x >> 9)
         lane = (x >> 2) & 127
-        total = jnp.sum(jnp.where(live, 1, 0), axis=0, keepdims=True)
-        heads = jnp.sum(jnp.where(live & (r < HALO), 1, 0), axis=0, keepdims=True)
-        tails = jnp.sum(jnp.where(live & (r >= 44), 1, 0), axis=0, keepdims=True)
-        last = band == 3
+        total = jnp.sum(jnp.where(live, 1, 0), axis=1, keepdims=True)
+        heads = jnp.sum(jnp.where(live & (r < HALO), 1, 0), axis=1, keepdims=True)
+        tails = jnp.sum(jnp.where(live & (r >= 44), 1, 0), axis=1, keepdims=True)
         if q == 0:
             row, first, many = r + HALO, jnp.zeros_like(total), total
         elif q == 1:
@@ -150,13 +148,24 @@
             first = jnp.where(last, total - tails, 0)
             many = jnp.where(last, tails, heads)
         e = half * EXT + row
-        slot = iota((32, 128), 0)
-        rot = (lane - iota((32, 128), 1)) & 127
-        key_v[q, 0:32, :] = ((tile * EXT + (e >> 1)) << 20) + (((e & 1) * 128 + lane) << 12) + (rot << 5) + slot
-        key_v[q, 32:40, :] = jnp.broadcast_to(first, (8, 128))
-        key_v[q, 40:48, :] = jnp.broadcast_to(many, (8, 128))
+        rot = (lane - iota((128, 128), 0)) & 127
+        key = ((tile * EXT + (e >> 1)) << 20) + (((e & 1) * 128 + lane) << 12) + ((spread & 31) << 7) + rot
+        for bit in range(5 if q else 0):
+            key = jnp.where((first >> bit) & 1 == 1, pltpu.roll(key, 128 - (1 << bit), axis=1), key)
+        key_v[q] = jnp.where(spread == 65, many, key)
     copy = pltpu.make_async_copy(key_v, key_s, sem)
     copy.start()
+    for q in range(3):
+        t = list_ref[q]
+        if q == 1:
+            t = jnp.where(band == 0, 0.0, t)
+        if q == 2:
+            t = jnp.where(last, list_ref[0], t)
+        t = t.T
+        dense[0:128, :] = t
+        dense[128:256, :] = t
+        for slot in range(32):
+            turned[q, slot * 8 : slot * 8 + 8, :] = dense[pl.ds(slot, 8, stride=32), :]
 
     def clear(i, c):
         acc[pl.ds(pl.multiple_of(i * 512, 512), 512), :] = jnp.zeros((512, 128), jnp.float32)
@@ -165,50 +174,66 @@
     lax.fori_loop(0, TRASH // 512, clear, 0)
     acc[TRASH : TRASH + 8, :] = jnp.zeros((8, 128), jnp.float32)
     copy.wait()
-    spot = iota((8, 128), 1) + 128 * (iota((8, 128), 0) >> 2)
+    spot = (iota((8, 128), 1) + 128 * (iota((8, 128), 0) >> 2)) << 12
+    flats = (flat0, flat1, flat2)
+    steps = (16, 5, 5)
+
+    def sender(i, at):
+        many = [key_s[q, i, 65] for q in range(3)]
+        read = [[key_s[q, i, v] for v in range(steps[q])] for q in range(3)]
+        for q in range(3):
+            for v, value in enumerate(read[q]):
+                flats[q][at[q] + v] = value
+        over = many[0] > steps[0]
+        for q in (1, 2):
+            over = over | (many[q] > steps[q])
+
+        def rest(j, c):
+            for q in range(3):
+                values = [key_s[q, i, v] for v in range(steps[q], 32)]
+                for v, value in enumerate(values):
+                    flats[q][at[q] + steps[q] + v] = value
+            return c
+
+        lax.fori_loop(0, over.astype(jnp.int32), rest, 0)
+        return tuple(a + m for a, m in zip(at, many))
+
+    sizes = lax.fori_loop(0, 128, sender, (jnp.int32(0),) * 3)
+
+    def finish(i, c):
+        for q in range(3):
+            flats[q][sizes[q] + i] = jnp.int32(((TRASH // 8) << 20) - (1 << 32))
+        return c
+
+    lax.fori_loop(0, 2 * UNROLL, finish, 0)
     for q in range(3):
-        step = 8 if q == 0 else 4
-
-        def sender(i, at, q=q, step=step):
-            first = key_s[q, 32, i]
-            many = key_s[q, 40, i]
-
-            def some(j, c):
-                for v in range(step):
-                    flat[at + j * step + v] = key_s[q, first + j * step + v, i]
-                return c
-
-            some(0, 0)
-            lax.fori_loop(1, (many + step - 1) // step, some, 0)
-            return at + many
-
-        size = lax.fori_loop(0, 128, sender, 0)
-
-        def finish(i, c, size=size):
-            flat[size + i] = jnp.int32(((TRASH // 8) << 20) - (1 << 32))
-            return c
-
-        lax.fori_loop(0, 2 * UNROLL, finish, 0)
 
         def prepare(j, q=q):
             bases, values = [], []
             for v in range(UNROLL):
-                key = flat[j * UNROLL + v]
-                bases.append(pl.multiple_of(lax.shift_right_logical(key, 20) * 8, 8))
-                target = lax.shift_right_logical(key, 12) & 255
-                charges = turned[q, pl.ds(key & 31, 8, stride=32), :]
-                moved = pltpu.roll(charges, (key >> 5) & 127, axis=1)
+                key = flats[q][j * UNROLL + v]
+                bases.append(lax.shift_right_logical(key, 20))
+                slot = pl.multiple_of((key >> 4) & 248, 8)
+                moved = pltpu.roll(turned[q, pl.ds(slot, 8), :], key & 127, axis=1)
+                target = jnp.full((8, 128), key, jnp.int32) & (255 << 12)
                 values.append(jnp.where(spot == target, moved, 0.0))
             return tuple(bases), tuple(values)
 
         def add(j, carry, prepare=prepare):
             bases, values = carry
             following = prepare(j + 1)
-            for base, value in zip(bases, values):
-                acc[pl.ds(pl.multiple_of(base, 8), 8), :] += value
+            for v in range(0, UNROLL, 4):
+                places = [pl.ds(pl.multiple_of(bases[v + w] * 8, 8), 8) for w in range(4)]
+                sums = [acc[place, :] + values[v + w] for w, place in enumerate(places)]
+                for w in range(1, 4):
+                    for z in range(w):
+                        same = bases[v + z] == bases[v + w]
+                        sums[w] = sums[w] + jnp.where(same, values[v + z], 0.0)
+                for place, value in zip(places, sums):
+                    acc[place, :] = value
             return following
 
-        lax.fori_loop(0, (size + UNROLL - 1) // UNROLL, add, prepare(0))
+        lax.fori_loop(0, (sizes[q] + UNROLL - 1) // UNROLL, add, prepare(0))
 
     def diffuse(which, carry):
         half = which >> 1
@@ -483,9 +508,12 @@
         out_specs=vmem,
         scratch_shapes=[
             pltpu.VMEM((TRASH + 8, 128), jnp.float32),
+            pltpu.VMEM((256, 128), jnp.float32),
             pltpu.VMEM((3, 256, 128), jnp.float32),
-            pltpu.VMEM((3, 48, 128), jnp.int32),
-            pltpu.SMEM((3, 48, 128), jnp.int32),
+            pltpu.VMEM((3, 128, 128), jnp.int32),
+            pltpu.SMEM((3, 128, 128), jnp.int32),
+            pltpu.SMEM((LIST,), jnp.int32),
+            pltpu.SMEM((LIST,), jnp.int32),
             pltpu.SMEM((LIST,), jnp.int32),
             pltpu.VMEM((7 * 192, WIDE), jnp.bfloat16),
             pltpu.VMEM((288, WIDE), jnp.float32),

time: 125 us -> 113 us (0.904)
  the two profiles are of different devices: /device:TPU:7 before, /device:TPU:3 now
where the time goes in v3:
time: 113 us
  Pallas kernels  105 us (93%)
  local copies, waits for them, and re-layouts  6.63 us (6%)
  other arithmetic  1.43 us (1%)
    pallas_call x1, Pallas kernels, shards(): pl.pallas_call(photons_to_readout, out_shape=jax.ShapeDtypeStruct((32, 32...  43.1 us
    pallas_call x1, Pallas kernels, shards(): pl.pallas_call(exchange_readout, out_shape=jax.ShapeDtypeStruct((32, 32,...  31.7 us
    pallas_call x1, Pallas kernels, shards(): pl.pallas_call(exchange_photons, out_shape=jax.ShapeDtypeStruct((3, 128,...  19.9 us
    pallas_call x1, Pallas kernels, shards(): pl.pallas_call(crosstalk_kernel, out_shape=jax.ShapeDtypeStruct((4096, 12...  4.37 us
    unnamed x4, local copies, waits for them, and re-layouts  4.09 us
    pallas_call x1, Pallas kernels, shards(): pl.pallas_call(tables, out_shape=[jax.ShapeDtypeStruct((2, 2, 288, 768),...  3.78 us

profile of v3, /device:TPU:3, one launch (start us, length us, event | category | flops | bytes accessed | tf_op | source)
XLA Modules:
  0.0 112.9 jit_solution(16038363496154192500)
XLA Ops:
  0.0 0.7 iota_compare_fusion
  0.7 0.8 copy.25
  1.5 0.1 copy.20
  1.6 0.8 copy.23
  2.4 0.1 rev.9
  2.5 0.7 reshape.53.base2_ref
  3.2 0.8 copy.21
  4.1 0.1 rev.8
  4.2 0.7 reshape.52.base1_ref
  4.9 0.8 copy.22
  5.8 0.7 pad_maximum_fusion.message_ref
  6.5 2.0 %shard_map.64 = f32[128,128]{1,0:T(8,128)} custom-call(f32[128,128]{1,0:T(8,128)} %pad_maximum_fusion.message_ref), custom_call_target="tpu_custom_call" | custom-call | tf_op jit(solution)/shard_map/pallas_call | solution.py:465
  8.5 19.9 %shard_map.65 = f32[3,128,1,128]{3,2,1,0:T(1,128)} custom-call(f32[128,1,128]{2,1,0:T(1,128)} %bitcast.29), custom_call_target="tpu_custom_call" | custom-call | tf_op jit(solution)/shard_map/pallas_call | solution.py:471
  28.3 1.6 %copy.26 = bf16[32,16,16]{2,1,0:T(8,128)(2,1)} copy(bf16[32,16,16]{0,2,1:T(8,128)(2,1)} %param.11) | data formatting | bytes 32768 | tf_op args[5]
  30.0 3.8 %shard_map.66 = (bf16[2,2,288,768]{3,2,1,0:T(8,128)(2,1)}, bf16[2,2,192,256]{3,2,1,0:T(8,128)(2,1)}, bf16[4,256,256]{2,1,0:T(8,128)(2,1)}) custom-call(s32[1]{0:T(128)} %bitcast.band_ref, f32[2,36,128]{2,1,0:T(8,128)} %reshape.52.base1_ref, f32[2,12,128]{2,1,0:T(8,128)} %reshape.53.base2_ref, bf16[512,16]{1,0:T(8,128)(2,1)} %bitcast.31), custom_call_target="tpu_custom_call" | custom-call | flops 100000000 | bytes 4000000 | tf_op jit(solution)/shard_map/pallas_call | solution.py:492
  33.8 43.1 %shard_map.67.block_ref = bf16[32,32,512]{2,1,0:T(8,128)(2,1)} custom-call(s32[1]{0:T(128)} %bitcast.band_ref, f32[3,128,128]{2,1,0:T(8,128)} %bitcast.28, bf16[2,2,288,768]{3,2,1,0:T(8,128)(2,1)} %get-tuple-element.8.w1_ref, bf16[2,2,192,256]{3,2,1,0:T(8,128)(2,1)} %get-tuple-element.9.w2_ref), custom_call_target="tpu_custom_call" | custom-call | tf_op jit(solution)/shard_map/pallas_call | solution.py:504
  76.8 31.7 %shard_map.68.got_ref = bf16[32,32,512]{2,1,0:T(8,128)(2,1)} custom-call(bf16[32,32,512]{2,1,0:T(8,128)(2,1)} %shard_map.67.block_ref), custom_call_target="tpu_custom_call" | custom-call | tf_op jit(solution)/shard_map/pallas_call | solution.py:527
  108.5 4.4 %shard_map.69 = f32[4096,128]{1,0:T(8,128)} custom-call(bf16[32,32,512]{2,1,0:T(8,128)(2,1)} %shard_map.68.got_ref, bf16[4,256,256]{2,1,0:T(8,128)(2,1)} %get-tuple-element.10.mix_ref), custom_call_target="tpu_custom_call" | custom-call | tf_op jit(solution)/shard_map/pallas_call | solution.py:535
  (10 shorter events, 0.1 us)
